TPU v7x, 256 devices: a whole 4x4x8 slice. The times are simulated.
256 devices in a mesh: dp: 64 (over z, y, core), tensor: 4 (over x).
Axes of the slice: x: 4, y: 4, z: 8, core: 2. Of those that a mesh axis runs over, the one named last changes fastest.
Arguments:
- tokens: bfloat16 [32768, 8192], P('dp', 'tensor'), may hold values from -6 to 6
- token_adapter_index: int32 [32768, 1], P('dp'), may hold values from 0 to 63; in each aligned block of 512 rows (0 to 511, 512 to 1023, ...) at most 16 rows name the same one
- frozen_key_value_weight: bfloat16 [8192, 2048], P('tensor'), may hold values from -0.0625 to 0.0625
- adapter_down_weight: bfloat16 [64, 64, 8192], P('dp', None, 'tensor'), may hold values from -0.0625 to 0.0625
- adapter_up_weight: bfloat16 [64, 64, 2048], P('dp', None, 'tensor'), may hold values from -0.75 to 0.75
Outputs:
- projected: bfloat16 [32768, 2048], P('dp', 'tensor')
Inputs may be any that keep to these rules, and one draw needn't show every extreme that they name: `token_adapter_index`: among the tokens of one index of dp, no adapter is named by more than 16 tokens, a bound that some block reaches.
All inputs are finite; a program needn't handle non-finite values.
Results may differ from a plain program's by a relative error of at most 0.0048.
Values may be sent and summed in bfloat16 or wider, within the bound.
No kernel may reach another device: no remote copies, remote signals or barrier semaphores. Data moves between devices by JAX's collectives and lax.ppermute only.
A program may use at most 128 MiB of HBM per device.

v0:
```python
import jax
import jax.numpy as jnp
from jax import lax
from jax.sharding import PartitionSpec as P


def on_device(
    tokens, token_adapter_index, frozen_key_value_weight, adapter_down_weight, adapter_up_weight
):
    holder_count = lax.axis_size("dp")
    token_count = tokens.shape[0]
    feature_count = tokens.shape[1]
    row_capacity = 2 * token_count // holder_count
    adapter_rank_width = adapter_down_weight.shape[1]
    adapter_of = token_adapter_index[:, 0]
    membership = (adapter_of[:, None] == jnp.arange(holder_count, dtype=jnp.int32)[None, :]).astype(
        jnp.int32
    )
    earlier = jnp.cumsum(membership, axis=0) - membership
    position = jnp.sum(earlier * membership, axis=1)
    adapter_slot_index = adapter_of * row_capacity + position
    send_buffer = (
        jnp.zeros((holder_count * row_capacity, feature_count), tokens.dtype)
        .at[adapter_slot_index]
        .set(tokens)
    )
    send_buffer = send_buffer.reshape(holder_count, row_capacity, feature_count)
    partial_value = jnp.dot(tokens, frozen_key_value_weight, preferred_element_type=jnp.float32)
    base_out = lax.psum_scatter(partial_value, "tensor", scatter_dimension=1, tiled=True)
    product = jnp.einsum(
        "acd,ard->acr",
        send_buffer,
        lax.all_gather(adapter_down_weight, "dp", axis=0, tiled=True),
        preferred_element_type=jnp.float32,
    )
    summed = lax.psum(product.reshape(holder_count, row_capacity * adapter_rank_width), "tensor")
    reduced_activations = summed.reshape(holder_count, row_capacity, adapter_rank_width).astype(
        jnp.bfloat16
    )
    adapter_delta = jnp.einsum(
        "flz,fzq->flq",
        reduced_activations,
        lax.all_gather(adapter_up_weight, "dp", axis=0, tiled=True),
        preferred_element_type=jnp.float32,
    ).astype(jnp.bfloat16)
    flattened_delta = adapter_delta.reshape(holder_count * row_capacity, adapter_delta.shape[2])[
        adapter_slot_index
    ]
    return (base_out + flattened_delta.astype(jnp.float32)).astype(jnp.bfloat16)


def solution(mesh):
    placed = (
        P("dp", "tensor"),
        P("dp", None),
        P("tensor", None),
        P("dp", None, "tensor"),
        P("dp", None, "tensor"),
    )
    return jax.shard_map(
        on_device, mesh=mesh, in_specs=placed, out_specs=P("dp", "tensor"), check_vma=False
    )
```

profile of v0, /device:TPU:1, one launch (start us, length us, event | category | flops | bytes accessed | tf_op | source)
XLA Modules:
  0.0 209.0 jit_solution(12527318570697684783)
XLA Ops:
  7.4 0.0 all-gather.3.cloned.1.call-start
  7.4 0.7 all-gather.3.cloned.1.call-update
  8.1 0.0 all-gather.5.cloned.1.call-start
  8.1 0.7 all-gather.5.cloned.1.call-update
  8.8 0.0 reduce-scatter.2.cloned.1.call-start
  8.9 10.5 %fusion.6 = f32[512,2048]{1,0:T(8,128)} fusion(bf16[512,2048]{1,0:T(8,128)(2,1)} %param.5, bf16[2048,2048]{1,0:T(8,128)(2,1)} %param.7), kind=kOutput, calls=%fused_computation.17 | convolution fusion | flops 4294967296 | bytes 14680064 | tf_op jit(solution)/shard_map/dot_general | solution.py:28
  19.4 0.0 copy-start
  19.4 0.0 reduce-scatter.2.cloned.1.call-update
  19.4 0.7 copy-done
  20.1 1.2 reduce-window.6
  21.3 0.2 slice_reduce_fusion
  21.5 0.1 fusion.4
  21.7 7.3 %scatter_custom_fusion = bf16[1024,2048]{1,0:T(8,128)(2,1)} fusion(s32[512]{0:T(512)S(1)} %bitcast.36, bf16[512,2048]{1,0:T(8,128)(2,1)} %param.5, bf16[]{:T(256)} %constant.4.clone.1), kind=kCustom, calls=%fused_computation.2 | custom fusion | bytes 4194816 | tf_op jit(solution)/shard_map/scatter | solution.py:25
  29.0 86.4 %all-gather.3.cloned.1.call-done = bf16[64,64,2048]{2,1,0:T(8,128)(2,1)} async-done(((bf16[1,64,2048]{2,1,0:T(8,128)(2,1)}), bf16[64,64,2048]{2,1,0:T(8,128)(2,1)}) %all-gather.3.cloned.1.call-update) | async-done | bytes 16777232 | tf_op jit(solution)/shard_map/all_gather | solution.py:33
  115.4 11.5 %fusion.7 = f32[64,16,64]{2,1,0:T(8,128)S(1)} fusion(bf16[64,16,2048]{2,1,0:T(8,128)(2,1)} %bitcast.32, bf16[64,64,2048]{2,1,0:T(8,128)(2,1)} %all-gather.3.cloned.1.call-done), kind=kOutput, calls=%fused_computation.18 | convolution fusion | flops 268435456 | bytes 21233664 | tf_op jit(solution)/shard_map/acd,ard->acr/dot_general | solution.py:30
  126.9 0.2 reshape.30
  127.0 16.6 %all-reduce.1 = bf16[64,1024]{1,0:T(8,128)(2,1)S(1)} all-reduce(f32[64,1024]{1,0:T(8,128)S(1)} %reshape.30), channel_id=1, replica_groups=mesh['dp'=64,'tensor'=4] {'tensor'}, use_global_device_ids=true, to_apply=%region_5.6 | all-reduce | flops 65536 | bytes 393216 | tf_op jit(solution)/shard_map/psum | solution.py:36
  143.7 0.2 convert_element_type.25
  143.9 50.7 %all-gather.5.cloned.1.call-done = bf16[64,64,512]{2,1,0:T(8,128)(2,1)} async-done(((bf16[1,64,512]{2,1,0:T(8,128)(2,1)}), bf16[64,64,512]{2,1,0:T(8,128)(2,1)}) %all-gather.5.cloned.1.call-update) | async-done | bytes 4194320 | tf_op jit(solution)/shard_map/all_gather | solution.py:43
  194.6 2.8 %convolution_convert_fusion = bf16[64,16,512]{2,1,0:T(8,128)(2,1)S(1)} fusion(bf16[64,16,64]{2,1,0:T(8,128)(2,1)S(1)} %convert_element_type.25, bf16[64,64,512]{2,1,0:T(8,128)(2,1)} %all-gather.5.cloned.1.call-done), kind=kOutput, calls=%fused_computation.4 | convolution fusion | flops 67633152 | bytes 5373952 | tf_op jit(solution)/shard_map/flz,fzq->flq/dot_general | solution.py:40
  197.4 2.0 gather_fusion
  199.4 0.0 reduce-scatter.2.cloned.1.call-done
  199.4 2.2 %add_convert_fusion = bf16[512,512]{1,0:T(8,128)(2,1)} fusion(f32[512,512]{1,0:T(8,128)} %reduce-scatter.2.cloned.1.call-done, bf16[512,512]{1,0:T(8,128)(2,1)S(1)} %gather_fusion), kind=kLoop, calls=%fused_computation.5 | loop fusion | flops 786432 | bytes 2097152 | tf_op jit(solution)/shard_map/convert_element_type | solution.py:49
  (5 shorter events, 0.1 us)
Async XLA Ops:
  7.4 108.0 %all-gather.3.cloned.1.call-start = ((), (), s32[]{:S(2)}) async-start(), calls=%async_computation.2 | async-start | bytes 17039360 | tf_op jit(solution)/shard_map/all_gather | solution.py:33
  8.1 186.5 %all-gather.5.cloned.1.call-start = ((), (), s32[]{:S(2)}) async-start(), calls=%async_computation.3 | async-start | bytes 4259840 | tf_op jit(solution)/shard_map/all_gather | solution.py:43
  8.8 190.6 %reduce-scatter.2.cloned.1.call-start = ((), (), s32[]{:S(2)}) async-start(), calls=%async_computation.1 | async-start | bytes 5242880 | tf_op jit(solution)/shard_map/reduce_scatter | solution.py:29
  19.4 0.7 copy-start
Sparse Core Ops, SparseCore 0:
  11.3 103.9 all-gather.2
  118.5 76.0 all-gather.4
Sparse Core Ops, SparseCore 1:
  19.5 53.0 reduce-scatter.1
where the time goes:
time: 209 us
  waiting for transfers between devices  139 us (67%)
  matrix products  24.8 us (12%)
  blocking collectives  16.6 us (8%)
  between operations  14.9 us (7%)
  local copies, waits for them, and re-layouts  10.5 us (5%)
  other arithmetic  3.57 us (2%)
    all_gather x1, waiting for transfers between devices, on_device(): lax.all_gather(adapter_down_weight, 'dp', axis=0, tiled=True)  86.4 us
    all_gather x1, waiting for transfers between devices, on_device(): lax.all_gather(adapter_up_weight, 'dp', axis=0, tiled=True)  50.7 us
    psum x1, blocking collectives, on_device(): lax.psum(product.reshape(holder_count, row_capacity * adapter_rank_width)...  16.6 us
    dot_general x1, matrix products, on_device(): jnp.einsum('acd,ard->acr', send_buffer, lax.all_gather(adapter_down_weigh...  11.5 us
    dot_general x1, matrix products, on_device(): jnp.dot(tokens, frozen_key_value_weight, preferred_element_type=jnp.float32)  10.5 us
    scatter x1, local copies, waits for them, and re-layouts, on_device(): send_buffer = jnp.zeros((holder_count * row_capacity, feature_count), tok...  7.26 us
  transfers between devices with their start and end apart: 3, of which 2 were waited for; matrix products, arithmetic and copies ran while one was open for 17% of the time, Pallas kernels for 0%

commit v1 on v0

--- a/solution.py
+++ b/solution.py
@@ -33,7 +33,8 @@
         lax.all_gather(adapter_down_weight, "dp", axis=0, tiled=True),
         preferred_element_type=jnp.float32,
     )
-    summed = lax.psum(product.reshape(holder_count, row_capacity * adapter_rank_width), "tensor")
+    vec = product.reshape(holder_count, row_capacity * adapter_rank_width)
+    summed = jnp.sum(lax.all_gather(vec, "tensor"), 0)
     reduced_activations = summed.reshape(holder_count, row_capacity, adapter_rank_width).astype(
         jnp.bfloat16
     )

time: 209 us -> 290 us (1.39)
  waiting for transfers between devices: 139 us -> 235 us
  blocking collectives: 16.6 us -> 0 us
  other arithmetic: 3.57 us -> 6.92 us
    reduce_scatter x1, waiting for transfers between devices: 0.03 us -> 43.8 us  [on_device(): lax.psum_scatter(partial_value, 'tensor', scatter_dimension=1, tiled=True)]
    all_gather x1, waiting for transfers between devices: 50.7 us -> 82 us  [on_device(): lax.all_gather(adapter_up_weight, 'dp', axis=0, tiled=True)]
    psum x1 -> x0, blocking collectives: 16.6 us -> none  [on_device(): lax.psum(product.reshape(holder_count, row_capacity * adapter_rank_width)...]
    all_gather x0 -> x1, waiting for transfers between devices: none -> 11.8 us  [on_device(): summed = jnp.sum(lax.all_gather(vec, 'tensor'), 0)]
    all_gather x1, waiting for transfers between devices: 86.4 us -> 96.1 us  [on_device(): lax.all_gather(adapter_down_weight, 'dp', axis=0, tiled=True)]
  transfers between devices with their start and end apart: 3 -> 4, of which waited for: 2 -> 4; matrix products, arithmetic and copies ran while one was open for 17% -> 9% of each run, Pallas kernels for 0% -> 0%
where the time goes in v1:
time: 290 us
  waiting for transfers between devices  235 us (81%)
  matrix products  24 us (8%)
  between operations  13.2 us (5%)
  local copies, waits for them, and re-layouts  10.5 us (4%)
  other arithmetic  6.92 us (2%)
    all_gather x1, waiting for transfers between devices, on_device(): lax.all_gather(adapter_down_weight, 'dp', axis=0, tiled=True)  96.1 us
    all_gather x1, waiting for transfers between devices, on_device(): lax.all_gather(adapter_up_weight, 'dp', axis=0, tiled=True)  82 us
    reduce_scatter x1, waiting for transfers between devices, on_device(): lax.psum_scatter(partial_value, 'tensor', scatter_dimension=1, tiled=True)  43.8 us
    all_gather x1, waiting for transfers between devices, on_device(): summed = jnp.sum(lax.all_gather(vec, 'tensor'), 0)  11.8 us
    dot_general x1, matrix products, on_device(): jnp.einsum('acd,ard->acr', send_buffer, lax.all_gather(adapter_down_weigh...  11.6 us
    dot_general x1, matrix products, on_device(): jnp.dot(tokens, frozen_key_value_weight, preferred_element_type=jnp.float32)  9.48 us
    scatter x1, local copies, waits for them, and re-layouts, on_device(): send_buffer = jnp.zeros((holder_count * row_capacity, feature_count), tok...  7.2 us
  transfers between devices with their start and end apart: 4, of which 4 were waited for; matrix products, arithmetic and copies ran while one was open for 9% of the time, Pallas kernels for 0%

profile of v1, /device:TPU:1, one launch (start us, length us, event | category | flops | bytes accessed | tf_op | source)
XLA Modules:
  0.0 290.1 jit_solution(17994868904363144154)
XLA Ops:
  6.5 0.0 all-gather.4.cloned.1.call-start
  6.5 0.7 all-gather.4.cloned.1.call-update
  7.3 0.0 all-gather.6.cloned.1.call-start
  7.3 0.7 fusion.5
  8.0 1.2 reduce-window.6
  9.2 0.2 slice_reduce_fusion
  9.5 0.8 fusion.4
  10.3 0.7 compare_select_fusion
  11.0 7.2 %scatter_custom_fusion = bf16[1024,2048]{1,0:T(8,128)(2,1)} fusion(s32[512]{0:T(512)S(1)} %bitcast.36, bf16[512,2048]{1,0:T(8,128)(2,1)} %param.5, bf16[]{:T(256)} %constant.5.clone.1), kind=kCustom, calls=%fused_computation.2 | custom fusion | bytes 4194816 | tf_op jit(solution)/shard_map/scatter | solution.py:25
  18.2 96.1 %all-gather.4.cloned.1.call-done = bf16[64,64,2048]{2,1,0:T(8,128)(2,1)} async-done(((bf16[1,64,2048]{2,1,0:T(8,128)(2,1)}), bf16[64,64,2048]{2,1,0:T(8,128)(2,1)}) %all-gather.4.cloned.1.call-update) | async-done | bytes 16777232 | tf_op jit(solution)/shard_map/all_gather | solution.py:33
  114.3 0.0 copy-start
  114.3 11.6 %fusion.7 = f32[64,16,64]{2,1,0:T(8,128)S(1)} fusion(bf16[64,16,2048]{2,1,0:T(8,128)(2,1)} %bitcast.32, bf16[64,64,2048]{2,1,0:T(8,128)(2,1)} %all-gather.4.cloned.1.call-done), kind=kOutput, calls=%fused_computation.18 | convolution fusion | flops 268435456 | bytes 21233664 | tf_op jit(solution)/shard_map/acd,ard->acr/dot_general | solution.py:30
  126.0 0.9 all_gather_reshape.3
  126.8 0.0 all-gather.6.cloned.1.call-update
  126.9 0.0 all-gather.8.cloned.1.call-start
  126.9 0.7 all-gather.8.cloned.1.call-update
  127.6 0.2 reduce-scatter.2.cloned.1.call-start
  127.8 0.0 copy-done
  127.8 9.5 %fusion.6 = f32[512,2048]{1,0:T(8,128)} fusion(bf16[512,2048]{1,0:T(8,128)(2,1)S(1)} %copy-done, bf16[2048,2048]{1,0:T(8,128)(2,1)} %param.7), kind=kOutput, calls=%fused_computation.17 | convolution fusion | flops 4294967296 | bytes 14680064 | tf_op jit(solution)/shard_map/dot_general | solution.py:28
  137.3 0.0 reduce-scatter.2.cloned.1.call-update
  137.4 11.8 %all-gather.6.cloned.1.call-done = f32[4,64,1024]{2,1,0:T(8,128)} async-done(((f32[1,64,1024]{2,1,0:T(8,128)}), f32[4,64,1024]{2,1,0:T(8,128)}) %all-gather.6.cloned.1.call-update) | async-done | bytes 1048592 | tf_op jit(solution)/shard_map/all_gather | solution.py:37
  149.2 1.3 reduce_sum.22
  150.5 0.2 convert_element_type.25
  150.7 82.0 %all-gather.8.cloned.1.call-done = bf16[64,64,512]{2,1,0:T(8,128)(2,1)} async-done(((bf16[1,64,512]{2,1,0:T(8,128)(2,1)}), bf16[64,64,512]{2,1,0:T(8,128)(2,1)}) %all-gather.8.cloned.1.call-update) | async-done | bytes 4194320 | tf_op jit(solution)/shard_map/all_gather | solution.py:44
  232.7 2.8 convolution_convert_fusion
  235.6 2.0 gather_fusion
  237.5 43.8 %reduce-scatter.2.cloned.1.call-done = f32[512,512]{1,0:T(8,128)} async-done(((f32[512,2048]{1,0:T(8,128)}), f32[512,512]{1,0:T(8,128)}) %reduce-scatter.2.cloned.1.call-update) | async-done | bytes 1048592 | tf_op jit(solution)/shard_map/reduce_scatter | solution.py:29
  281.4 2.2 add_convert_fusion
  (3 shorter events, 0.0 us)
Async XLA Ops:
  6.5 107.8 %all-gather.4.cloned.1.call-start = ((), (), s32[]{:S(2)}) async-start(), calls=%async_computation.2 | async-start | bytes 17039360 | tf_op jit(solution)/shard_map/all_gather | solution.py:33
  7.3 141.9 %all-gather.6.cloned.1.call-start = ((), (), s32[]{:S(2)}) async-start(), calls=%async_computation.3 | async-start | bytes 1310720 | tf_op jit(solution)/shard_map/all_gather | solution.py:37
  114.3 13.5 %copy-start = (bf16[512,2048]{1,0:T(8,128)(2,1)S(1)}, bf16[512,2048]{1,0:T(8,128)(2,1)}, u32[]{:S(2)}) copy-start(bf16[512,2048]{1,0:T(8,128)(2,1)} %param.5) | copy-start | bytes 6291460
  126.9 105.8 %all-gather.8.cloned.1.call-start = ((), (), s32[]{:S(2)}) async-start(), calls=%async_computation.4 | async-start | bytes 4259840 | tf_op jit(solution)/shard_map/all_gather | solution.py:44
  127.6 153.8 %reduce-scatter.2.cloned.1.call-start = ((), (), s32[]{:S(2)}) async-start(), calls=%async_computation.1 | async-start | bytes 5242880 | tf_op jit(solution)/shard_map/reduce_scatter | solution.py:29
Sparse Core Ops, SparseCore 0:
  10.1 104.1 all-gather.3
  127.0 22.1 all-gather.5
  152.0 80.6 all-gather.7
  235.1 46.2 reduce-scatter.1

commit v2 on v0

--- a/solution.py
+++ b/solution.py
@@ -2,6 +2,11 @@
 import jax.numpy as jnp
 from jax import lax
 from jax.sharding import PartitionSpec as P
+
+
+def swapped_in(value, axis, dim):
+    outgoing = jnp.stack([value] * lax.axis_size(axis))
+    return jnp.concatenate(lax.all_to_all(outgoing, axis, 0, 0), axis=dim)
 
 
 def on_device(
@@ -30,7 +35,7 @@
     product = jnp.einsum(
         "acd,ard->acr",
         send_buffer,
-        lax.all_gather(adapter_down_weight, "dp", axis=0, tiled=True),
+        swapped_in(adapter_down_weight, "dp", 0),
         preferred_element_type=jnp.float32,
     )
     summed = lax.psum(product.reshape(holder_count, row_capacity * adapter_rank_width), "tensor")

time: 209 us -> 458 us (2.19)
  the two profiles are of different devices: /device:TPU:1 before, /device:TPU:48 now
where the time goes in v2:
time: 458 us; the launch traced here: 457 us
  waiting for transfers between devices  367 us (80%)
  matrix products  23.8 us (5%)
  blocking collectives  20 us (4%)
  local copies, waits for them, and re-layouts  16.1 us (4%)
  between operations  14.9 us (3%)
  starting transfers between devices  11.9 us (3%)
    all_to_all x1, waiting for transfers between devices, swapped_in(): return jnp.concatenate(lax.all_to_all(outgoing, axis, 0, 0), axis=dim)  366 us
    psum x1, blocking collectives, on_device(): lax.psum(product.reshape(holder_count, row_capacity * adapter_rank_width)...  20 us
    all_to_all x1, starting transfers between devices, swapped_in(): return jnp.concatenate(lax.all_to_all(outgoing, axis, 0, 0), axis=dim)  11.9 us
    dot_general x1, matrix products, on_device(): jnp.einsum('acd,ard->acr', send_buffer, swapped_in(adapter_down_weight, '...  11.5 us
    dot_general x1, matrix products, on_device(): jnp.dot(tokens, frozen_key_value_weight, preferred_element_type=jnp.float32)  9.44 us
  transfers between devices with their start and end apart: 3, of which 1 were waited for; matrix products, arithmetic and copies ran while one was open for 7% of the time, Pallas kernels for 0%

profile of v2, /device:TPU:48, one launch (start us, length us, event | category | flops | bytes accessed | tf_op | source)
XLA Modules:
  0.0 457.2 jit_solution(5055019261513162043)
XLA Ops:
  7.4 6.7 %stack.2 = bf16[64,1,64,2048]{3,2,1,0:T(8,128)(2,1)} broadcast(bf16[64,2048]{1,0:T(8,128)(2,1)} %bitcast.36), dimensions={2,3} | broadcast | bytes 17039360 | tf_op jit(solution)/shard_map/stack | solution.py:8
  14.1 0.0 copy-start.1
  14.1 11.9 %all-to-all-start = ((bf16[64,1,64,2048]{3,2,1,0:T(8,128)(2,1)}), bf16[64,1,64,2048]{3,2,1,0:T(8,128)(2,1)}, u32[]{:S(2)}, u32[]{:S(2)}) async-start(bf16[64,1,64,2048]{3,2,1,0:T(8,128)(2,1)} %stack.2), calls=%async_computation.1 | async-start | bytes 33554432 | tf_op jit(solution)/shard_map/all_to_all | solution.py:9
  25.9 0.0 all-gather.2.cloned.1.call-start
  26.0 0.7 all-gather.2.cloned.1.call-update
  26.7 0.0 reduce-scatter.2.cloned.1.call-start
  26.7 0.0 copy-done.1
  26.7 9.4 %fusion.8 = f32[512,2048]{1,0:T(8,128)} fusion(bf16[512,2048]{1,0:T(8,128)(2,1)S(1)} %copy-done.1, bf16[2048,2048]{1,0:T(8,128)(2,1)} %param.7), kind=kOutput, calls=%fused_computation.19 | convolution fusion | flops 4294967296 | bytes 14680064 | tf_op jit(solution)/shard_map/dot_general | solution.py:33
  36.2 0.0 copy-start
  36.2 0.0 reduce-scatter.2.cloned.1.call-update
  36.2 0.7 copy-done
  36.9 1.2 reduce-window.6
  38.1 0.2 slice_reduce_fusion
  38.3 0.1 fusion.6
  38.5 6.2 %scatter_custom_fusion = bf16[1024,2048]{1,0:T(8,128)(2,1)} fusion(s32[512]{0:T(512)S(1)} %bitcast.40, bf16[512,2048]{1,0:T(8,128)(2,1)S(1)} %copy-done.1, bf16[]{:T(256)} %constant.4.clone.1), kind=kCustom, calls=%fused_computation.4 | custom fusion | bytes 4194306 | tf_op jit(solution)/shard_map/scatter | solution.py:30
  44.6 366.1 %all-to-all-done = bf16[64,1,64,2048]{3,2,1,0:T(8,128)(2,1)} async-done(((bf16[64,1,64,2048]{3,2,1,0:T(8,128)(2,1)}), bf16[64,1,64,2048]{3,2,1,0:T(8,128)(2,1)}, u32[]{:S(2)}, u32[]{:S(2)}) %all-to-all-start) | async-done | bytes 16777248 | tf_op jit(solution)/shard_map/all_to_all | solution.py:9
  410.8 11.5 %fusion = f32[64,16,64]{2,1,0:T(8,128)S(1)} fusion(bf16[64,16,2048]{2,1,0:T(8,128)(2,1)} %bitcast.35, bf16[64,1,64,2048]{3,2,1,0:T(8,128)(2,1)} %all-to-all-done), kind=kOutput, calls=%fused_computation.2 | convolution fusion | flops 268435456 | bytes 21233664 | tf_op jit(solution)/shard_map/acd,ard->acr/dot_general | solution.py:35
  422.3 0.2 reshape.37
  422.5 20.0 %all-reduce.1 = bf16[64,1024]{1,0:T(8,128)(2,1)S(1)} all-reduce(f32[64,1024]{1,0:T(8,128)S(1)} %reshape.37), channel_id=1, replica_groups=mesh['dp'=64,'tensor'=4] {'tensor'}, use_global_device_ids=true, to_apply=%region_5.6 | all-reduce | flops 65536 | bytes 393216 | tf_op jit(solution)/shard_map/psum | solution.py:41
  442.5 0.2 convert_element_type.25
  442.6 0.0 all-gather.2.cloned.1.call-done
  442.7 2.8 convolution_convert_fusion
  445.5 2.0 gather_fusion
  447.5 0.0 reduce-scatter.2.cloned.1.call-done
  447.5 2.2 add_convert_fusion
  (5 shorter events, 0.1 us)
Async XLA Ops:
  14.1 12.7 %copy-start.1 = (bf16[512,2048]{1,0:T(8,128)(2,1)S(1)}, bf16[512,2048]{1,0:T(8,128)(2,1)}, u32[]{:S(2)}) copy-start(bf16[512,2048]{1,0:T(8,128)(2,1)} %param.5) | copy-start | bytes 6291460
  14.1 396.7 %all-to-all-start = ((bf16[64,1,64,2048]{3,2,1,0:T(8,128)(2,1)}), bf16[64,1,64,2048]{3,2,1,0:T(8,128)(2,1)}, u32[]{:S(2)}, u32[]{:S(2)}) async-start(bf16[64,1,64,2048]{3,2,1,0:T(8,128)(2,1)} %stack.2), calls=%async_computation.1 | async-start | bytes 33554432 | tf_op jit(solution)/shard_map/all_to_all | solution.py:9
  25.9 416.7 %all-gather.2.cloned.1.call-start = ((), (), s32[]{:S(2)}) async-start(), calls=%async_computation.3 | async-start | bytes 4259840 | tf_op jit(solution)/shard_map/all_gather | solution.py:48
  26.7 420.9 %reduce-scatter.2.cloned.1.call-start = ((), (), s32[]{:S(2)}) async-start(), calls=%async_computation.2 | async-start | bytes 5242880 | tf_op jit(solution)/shard_map/reduce_scatter | solution.py:34
  36.2 0.7 copy-start
Sparse Core Ops, SparseCore 0:
  29.9 145.4 all-gather.1
Sparse Core Ops, SparseCore 1:
  36.3 50.4 reduce-scatter.1
